TPU v7x, 32 devices: a whole 2x2x4 slice. The times are simulated.
32 devices in a mesh: member: 2 (over y), tile: 4 (over z), day: 4 (over x, core).
Axes of the slice: x: 2, y: 2, z: 4, core: 2. Of those that a mesh axis runs over, the one named last changes fastest.
Arguments:
- fields: bfloat16 [64, 35, 16384], P(('member', 'day'), None, 'tile'), parts along dimension 0, may hold values from -6 to 6
- remap_tiles: bfloat16 [512, 128, 128], P('tile'), may hold values from 0 to 0.015625
- tile_source: int32 [512], P('tile'), may hold values from 0 to 31, as said below
- tile_band: int32 [512, 1], P('tile'), may hold values from 0 to 3, as said below
- tile_block: int32 [512], P('tile'), may hold values from 0 to 35, as said below
- patterns: bfloat16 [18432, 512], P('tile'), may hold values from -0.125 to 0.125
Outputs:
- scores: float32 [64, 35, 512], P(('member', 'day'), None, 'tile'), parts along dimension 0
There are 2 independent parts, one for each index of `member`. A program takes and returns all parts, laid end to end along the dimension named above; an argument that names none is the same for every part. Nothing has to cross between parts.
Inputs may be any that keep to these rules, and one draw needn't show every extreme that they name: `tile_source`: index of the source block, among the 32 blocks held by the tile's own device; each of those blocks is read by some tile of that device. `tile_band`: among the 128 tiles of one device, at most 64 go to one band, and in some device exactly 64 do. `tile_block`: every target block of every band is written by at least one tile.
All inputs are finite; a program needn't handle non-finite values.
Results may differ from a plain program's by a relative error of at most 0.0039.
Values may be sent and summed in bfloat16 or wider, within the bound.
No kernel may reach another device: no remote copies, remote signals or barrier semaphores. Data moves between devices by JAX's collectives and lax.ppermute only.
A program may use at most 128 MiB of HBM per device.

v0:
```python
import jax
import jax.numpy as jnp
from jax import lax
from jax.sharding import PartitionSpec as P


def on_device(fields, remap_tiles, tile_source, tile_band, tile_block, patterns):
    band_count = lax.axis_size("tile")
    day_count, var_count, source_cells = fields.shape
    tile_count, block_size, _ = remap_tiles.shape
    row_count = day_count * var_count
    source_blocks = source_cells // block_size
    target_blocks = patterns.shape[0] // block_size
    pattern_count = patterns.shape[1]
    pattern_share = pattern_count // band_count
    capacity = max(2, 2 * tile_count // band_count)
    slot_count = band_count * capacity
    blocked = fields.reshape(row_count, source_blocks, block_size)
    columns = jnp.take(blocked, tile_source, axis=1)
    owner = tile_band[:, 0]
    tile_order = jnp.arange(tile_count, dtype=jnp.int32)
    same_owner = owner[:, None] == owner[None, :]
    earlier = tile_order[:, None] > tile_order[None, :]
    rank_within = jnp.sum(jnp.logical_and(same_owner, earlier).astype(jnp.int32), axis=1)
    slot_index = owner * capacity + rank_within
    block_label = (
        jnp.full((slot_count,), -1.0, jnp.bfloat16)
        .at[slot_index]
        .set(tile_block.astype(jnp.bfloat16))
    )
    contrib = jnp.einsum(
        "rtk,tkj->trj", columns, remap_tiles, preferred_element_type=jnp.float32
    ).astype(jnp.bfloat16)
    send_values = (
        jnp.zeros((slot_count, row_count, block_size), jnp.bfloat16).at[slot_index].set(contrib)
    )
    received, label_recv = (
        lax.all_to_all(send_values, "tile", split_axis=0, concat_axis=0, tiled=True),
        lax.all_to_all(block_label, "tile", split_axis=0, concat_axis=0, tiled=True),
    )
    block_ids = jnp.arange(target_blocks, dtype=jnp.int32).astype(jnp.bfloat16)
    selector = (label_recv[None, :] == block_ids[:, None]).astype(jnp.bfloat16)
    remapped = jnp.einsum("bs,srk->rbk", selector, received, preferred_element_type=jnp.float32)
    remapped = remapped.astype(jnp.bfloat16).reshape(row_count, target_blocks * block_size)
    partial_scores = jnp.dot(remapped, patterns, preferred_element_type=jnp.float32)
    total_scores = lax.psum(partial_scores, "tile")
    own_scores = lax.dynamic_slice_in_dim(
        total_scores, lax.axis_index("tile") * pattern_share, pattern_share, 1
    )
    return own_scores.reshape(day_count, var_count, pattern_share)


def solution(mesh):
    return jax.shard_map(
        on_device,
        mesh=mesh,
        in_specs=(
            P(("member", "day"), None, "tile"),
            P("tile", None, None),
            P("tile"),
            P("tile", None),
            P("tile"),
            P("tile", None),
        ),
        out_specs=P(("member", "day"), None, "tile"),
        check_vma=False,
    )
```

profile of v0, /device:TPU:0, one launch (start us, length us, event | category | flops | bytes accessed | tf_op | source)
XLA Modules:
  0.0 542.6 jit_solution(3007958193052604485)
XLA Ops:
  6.5 0.9 convert_reduce_fusion
  7.4 0.7 fusion.21
  8.1 0.7 convert_element_type.25
  8.8 1.3 scatter_custom_fusion.1
  10.1 0.7 all_to_all.12
  10.8 6.3 %all-to-all-start.1 = ((bf16[4,64,1]{1,2,0:T(2,128)(2,1)}), bf16[4,64,1]{1,2,0:T(2,128)(2,1)S(1)}, u32[]{:S(2)}, u32[]{:S(2)}) async-start(bf16[4,64,1]{1,2,0:T(2,128)(2,1)} %all_to_all.12), calls=%async_computation.1 | async-start | bytes 4096 | tf_op jit(solution)/shard_map/all_to_all | solution.py:39
  17.1 0.7 compare_select_fusion
  17.8 0.7 compare_and_fusion
  18.4 2.9 copy.16
  21.4 2.6 reshape.24
  24.0 2.5 copy.17
  26.5 7.1 %gather_fusion = bf16[128,280,128]{2,1,0:T(8,128)(2,1)} fusion(bf16[280,32,128]{2,0,1:T(8,128)(2,1)S(1)} %copy.17, s32[1024]{0:T(1024)S(1)} %pad_clamp_fusion), kind=kCustom, calls=%fused_computation | custom fusion | bytes 18350592 | tf_op jit(solution)/shard_map/jit(_take)/gather | solution.py:19
  33.6 13.4 %fusion.6 = bf16[128,280,128]{2,1,0:T(8,128)(2,1)} fusion(bf16[128,128,128]{2,1,0:T(8,128)(2,1)} %param.7, bf16[128,280,128]{2,1,0:T(8,128)(2,1)} %gather_fusion, pred[128]{0:T(512)(128)(4,1)S(1)} %compare_and_fusion), kind=kOutput, calls=%fused_computation.9 | convolution fusion | flops 1183580160 | bytes 22544512 | tf_op jit(solution)/shard_map/rtk,tkj->trj/dot_general | solution.py:31
  47.0 6.6 %broadcast_in_dim.24 = bf16[256,280,128]{2,1,0:T(8,128)(2,1)} broadcast(bf16[]{:T(256)} %constant.12.clone.1), dimensions={} | broadcast | bytes 18350082 | tf_op jit(solution)/shard_map/broadcast_in_dim | solution.py:35
  53.5 24.0 %scatter_fusion = bf16[256,280,128]{2,1,0:T(8,128)(2,1)} fusion(bf16[256,280,128]{2,1,0:T(8,128)(2,1)} %broadcast_in_dim.24, s32[128]{0:T(128)S(1)} %fusion.21, bf16[128,280,128]{2,1,0:T(8,128)(2,1)} %fusion.6), kind=kCustom, calls=%fused_computation.1 | custom fusion | bytes 27525632 | tf_op jit(solution)/shard_map/scatter | solution.py:35
  77.5 0.0 all-to-all-done.1
  77.5 7.3 %all-to-all-start = ((bf16[256,280,128]{2,1,0:T(8,128)(2,1)}), bf16[256,280,128]{2,1,0:T(8,128)(2,1)}, u32[]{:S(2)}, u32[]{:S(2)}) async-start(bf16[256,280,128]{2,1,0:T(8,128)(2,1)} %scatter_fusion), calls=%async_computation | async-start | bytes 36700160 | tf_op jit(solution)/shard_map/all_to_all | solution.py:38
  84.8 0.2 all-reduce.2.cloned.1.call-start
  85.1 0.1 eq.34
  85.2 396.5 %all-to-all-done = bf16[256,280,128]{2,1,0:T(8,128)(2,1)} async-done(((bf16[256,280,128]{2,1,0:T(8,128)(2,1)}), bf16[256,280,128]{2,1,0:T(8,128)(2,1)}, u32[]{:S(2)}, u32[]{:S(2)}) %all-to-all-start) | async-done | bytes 18350112 | tf_op jit(solution)/shard_map/all_to_all | solution.py:38
  481.7 9.4 %fusion.13 = bf16[280,128,36]{1,2,0:T(8,128)(2,1)S(1)} fusion(bf16[256,280,128]{2,1,0:T(8,128)(2,1)} %all-to-all-done, bf16[256]{0:T(256)(128)(2,1)S(1)} %eq.34, bf16[36]{0:T(256)(128)(2,1)S(1)} %iota_convert_fusion), kind=kOutput, calls=%fused_computation.14 | convolution fusion | flops 661902336 | bytes 20931144 | tf_op jit(solution)/shard_map/bs,srk->rbk/dot_general | solution.py:43
  491.2 4.7 fusion.10
  495.8 0.0 all-reduce.2.cloned.1.call-update
  495.9 38.3 %all-reduce.2.cloned.1.call-done = f32[280,512]{1,0:T(8,128)} async-done(((f32[280,512]{1,0:T(8,128)}), f32[280,512]{1,0:T(8,128)}) %all-reduce.2.cloned.1.call-update) | async-done | bytes 573456 | tf_op jit(solution)/shard_map/psum | solution.py:46
  534.1 0.9 constant_dynamic-slice_fusion
  535.1 0.7 copy.20
  (4 shorter events, 0.0 us)
Async XLA Ops:
  10.8 66.7 %all-to-all-start.1 = ((bf16[4,64,1]{1,2,0:T(2,128)(2,1)}), bf16[4,64,1]{1,2,0:T(2,128)(2,1)S(1)}, u32[]{:S(2)}, u32[]{:S(2)}) async-start(bf16[4,64,1]{1,2,0:T(2,128)(2,1)} %all_to_all.12), calls=%async_computation.1 | async-start | bytes 4096 | tf_op jit(solution)/shard_map/all_to_all | solution.py:39
  77.5 404.2 %all-to-all-start = ((bf16[256,280,128]{2,1,0:T(8,128)(2,1)}), bf16[256,280,128]{2,1,0:T(8,128)(2,1)}, u32[]{:S(2)}, u32[]{:S(2)}) async-start(bf16[256,280,128]{2,1,0:T(8,128)(2,1)} %scatter_fusion), calls=%async_computation | async-start | bytes 36700160 | tf_op jit(solution)/shard_map/all_to_all | solution.py:38
  84.8 449.3 %all-reduce.2.cloned.1.call-start = ((), (), s32[]{:S(2)}) async-start(), calls=%async_computation.2 | async-start | bytes 1146880 | tf_op jit(solution)/shard_map/psum | solution.py:46
Sparse Core Ops, SparseCore 0:
  496.0 38.1 all-reduce.1
where the time goes:
time: 543 us
  waiting for transfers between devices  435 us (80%)
  local copies, waits for them, and re-layouts  49.4 us (9%)
  matrix products  27.5 us (5%)
  starting transfers between devices  13.8 us (3%)
  between operations  13.5 us (2%)
    all_to_all x1, waiting for transfers between devices, on_device(): lax.all_to_all(send_values, 'tile', split_axis=0, concat_axis=0, tiled=True)  397 us
    psum x1, waiting for transfers between devices, on_device(): total_scores = lax.psum(partial_scores, 'tile')  38.3 us
    scatter x1, local copies, waits for them, and re-layouts, on_device(): jnp.zeros((slot_count, row_count, block_size), jnp.bfloat16).at[slot_index]  24 us
    dot_general x1, matrix products, on_device(): jnp.einsum('rtk,tkj->trj', columns, remap_tiles, preferred_element_type=j...  13.4 us
  transfers between devices with their start and end apart: 3, of which 2 were waited for; matrix products, arithmetic and copies ran while one was open for 11% of the time, Pallas kernels for 0%

commit v1 on v0

--- a/solution.py
+++ b/solution.py
@@ -1,7 +1,26 @@
+import functools
 import jax
 import jax.numpy as jnp
 from jax import lax
 from jax.sharding import PartitionSpec as P
+
+
+def post_shelves(x_in, mesh_name):
+    n_parts = lax.axis_size(mesh_name)
+
+    def _recast_halves(mixed_arr, later):
+        if later >= n_parts:
+            return mixed_arr
+        a_now = tuple(((dev_i, dev_i ^ later) for dev_i in range(n_parts)))
+        x_now = lax.ppermute(mixed_arr, mesh_name, a_now)
+        all_values = _recast_halves(mixed_arr + x_now, 2 * later)
+        return all_values
+
+    found_now = _recast_halves(x_in, 1)
+    return found_now
+
+
+handle_the_sector = functools.partial(post_shelves, mesh_name="tile")
 
 
 def on_device(fields, remap_tiles, tile_source, tile_band, tile_block, patterns):
@@ -43,7 +62,7 @@
     remapped = jnp.einsum("bs,srk->rbk", selector, received, preferred_element_type=jnp.float32)
     remapped = remapped.astype(jnp.bfloat16).reshape(row_count, target_blocks * block_size)
     partial_scores = jnp.dot(remapped, patterns, preferred_element_type=jnp.float32)
-    total_scores = lax.psum(partial_scores, "tile")
+    total_scores = handle_the_sector(partial_scores)
     own_scores = lax.dynamic_slice_in_dim(
         total_scores, lax.axis_index("tile") * pattern_share, pattern_share, 1
     )

time: 543 us -> 531 us (0.978)
  between operations: 13.5 us -> 0.11 us
    ppermute x0 -> x2, waiting for transfers between devices: none -> 40.3 us  [_recast_halves(): x_now = lax.ppermute(mixed_arr, mesh_name, a_now)]
    psum x1 -> x0, waiting for transfers between devices: 38.3 us -> none  [on_device(): total_scores = lax.psum(partial_scores, 'tile')]
  transfers between devices with their start and end apart: 3 -> 4, of which waited for: 2 -> 3; matrix products, arithmetic and copies ran while one was open for 11% -> 11% of each run, Pallas kernels for 0% -> 0%
where the time goes in v1:
time: 531 us; the launch traced here: 530 us
  waiting for transfers between devices  437 us (82%)
  local copies, waits for them, and re-layouts  48.5 us (9%)
  matrix products  26.7 us (5%)
  starting transfers between devices  13.9 us (3%)
    all_to_all x1, waiting for transfers between devices, on_device(): lax.all_to_all(send_values, 'tile', split_axis=0, concat_axis=0, tiled=True)  397 us
    ppermute x2, waiting for transfers between devices, _recast_halves(): x_now = lax.ppermute(mixed_arr, mesh_name, a_now)  40.3 us
    scatter x1, local copies, waits for them, and re-layouts, on_device(): jnp.zeros((slot_count, row_count, block_size), jnp.bfloat16).at[slot_index]  24 us
    dot_general x1, matrix products, on_device(): jnp.einsum('rtk,tkj->trj', columns, remap_tiles, preferred_element_type=j...  13.4 us
  transfers between devices with their start and end apart: 4, of which 3 were waited for; matrix products, arithmetic and copies ran while one was open for 11% of the time, Pallas kernels for 0%

profile of v1, /device:TPU:0, one launch (start us, length us, event | category | flops | bytes accessed | tf_op | source)
XLA Modules:
  0.0 530.0 jit_solution(2069957538258749205)
XLA Ops:
  0.0 0.9 convert_reduce_fusion
  0.9 0.7 fusion.21
  1.6 0.7 convert_element_type.25
  2.2 1.3 scatter_custom_fusion.1
  3.6 0.7 all_to_all.12
  4.2 6.3 %all-to-all-start.1 = ((bf16[4,64,1]{1,2,0:T(2,128)(2,1)}), bf16[4,64,1]{1,2,0:T(2,128)(2,1)S(1)}, u32[]{:S(2)}, u32[]{:S(2)}) async-start(bf16[4,64,1]{1,2,0:T(2,128)(2,1)} %all_to_all.12), calls=%async_computation.1 | async-start | bytes 4096 | tf_op jit(solution)/shard_map/all_to_all | solution.py:58
  10.6 0.7 compare_select_fusion
  11.2 0.7 compare_and_fusion
  11.9 2.9 copy.16
  14.8 2.6 reshape.24
  17.4 2.5 copy.17
  20.0 7.1 %gather_fusion = bf16[128,280,128]{2,1,0:T(8,128)(2,1)} fusion(bf16[280,32,128]{2,0,1:T(8,128)(2,1)S(1)} %copy.17, s32[1024]{0:T(1024)S(1)} %pad_clamp_fusion), kind=kCustom, calls=%fused_computation | custom fusion | bytes 18350592 | tf_op jit(solution)/shard_map/jit(_take)/gather | solution.py:38
  27.1 13.4 %fusion.6 = bf16[128,280,128]{2,1,0:T(8,128)(2,1)} fusion(bf16[128,128,128]{2,1,0:T(8,128)(2,1)} %param.7, bf16[128,280,128]{2,1,0:T(8,128)(2,1)} %gather_fusion, pred[128]{0:T(512)(128)(4,1)S(1)} %compare_and_fusion), kind=kOutput, calls=%fused_computation.9 | convolution fusion | flops 1183580160 | bytes 22544512 | tf_op jit(solution)/shard_map/rtk,tkj->trj/dot_general | solution.py:50
  40.4 6.6 %broadcast_in_dim.24 = bf16[256,280,128]{2,1,0:T(8,128)(2,1)} broadcast(bf16[]{:T(256)} %constant.12.clone.1), dimensions={} | broadcast | bytes 18350082 | tf_op jit(solution)/shard_map/broadcast_in_dim | solution.py:54
  47.0 24.0 %scatter_fusion = bf16[256,280,128]{2,1,0:T(8,128)(2,1)} fusion(bf16[256,280,128]{2,1,0:T(8,128)(2,1)} %broadcast_in_dim.24, s32[128]{0:T(128)S(1)} %fusion.21, bf16[128,280,128]{2,1,0:T(8,128)(2,1)} %fusion.6), kind=kCustom, calls=%fused_computation.1 | custom fusion | bytes 27525632 | tf_op jit(solution)/shard_map/scatter | solution.py:54
  71.0 0.0 all-to-all-done.1
  71.0 7.5 %all-to-all-start = ((bf16[256,280,128]{2,1,0:T(8,128)(2,1)}), bf16[256,280,128]{2,1,0:T(8,128)(2,1)}, u32[]{:S(2)}, u32[]{:S(2)}) async-start(bf16[256,280,128]{2,1,0:T(8,128)(2,1)} %scatter_fusion), calls=%async_computation | async-start | bytes 36700160 | tf_op jit(solution)/shard_map/all_to_all | solution.py:57
  78.5 0.1 eq.34
  78.6 396.8 %all-to-all-done = bf16[256,280,128]{2,1,0:T(8,128)(2,1)} async-done(((bf16[256,280,128]{2,1,0:T(8,128)(2,1)}), bf16[256,280,128]{2,1,0:T(8,128)(2,1)}, u32[]{:S(2)}, u32[]{:S(2)}) %all-to-all-start) | async-done | bytes 18350112 | tf_op jit(solution)/shard_map/all_to_all | solution.py:57
  475.4 9.4 %fusion.13 = bf16[280,128,36]{1,2,0:T(8,128)(2,1)S(1)} fusion(bf16[256,280,128]{2,1,0:T(8,128)(2,1)} %all-to-all-done, bf16[256]{0:T(256)(128)(2,1)S(1)} %eq.34, bf16[36]{0:T(256)(128)(2,1)S(1)} %iota_convert_fusion), kind=kOutput, calls=%fused_computation.14 | convolution fusion | flops 661902336 | bytes 20931144 | tf_op jit(solution)/shard_map/bs,srk->rbk/dot_general | solution.py:62
  484.8 3.8 fusion.10
  488.7 0.1 collective-permute-start
  488.7 14.0 %collective-permute-done = f32[280,512]{1,0:T(8,128)S(1)} collective-permute-done((f32[280,512]{1,0:T(8,128)S(1)}, f32[280,512]{1,0:T(8,128)S(1)}, u32[]{:S(2)}, u32[]{:S(2)}) %collective-permute-start) | collective-permute-done | bytes 573472 | tf_op jit(solution)/shard_map/ppermute | solution.py:15
  502.8 0.1 add.30
  502.8 0.1 collective-permute-start.1
  502.9 26.3 %collective-permute-done.1 = f32[280,512]{1,0:T(8,128)S(1)} collective-permute-done((f32[280,512]{1,0:T(8,128)S(1)}, f32[280,512]{1,0:T(8,128)S(1)}, u32[]{:S(2)}, u32[]{:S(2)}) %collective-permute-start.1) | collective-permute-done | bytes 573472 | tf_op jit(solution)/shard_map/ppermute | solution.py:15
  529.3 0.7 copy.20
  (5 shorter events, 0.1 us)
Async XLA Ops:
  4.2 66.7 %all-to-all-start.1 = ((bf16[4,64,1]{1,2,0:T(2,128)(2,1)}), bf16[4,64,1]{1,2,0:T(2,128)(2,1)S(1)}, u32[]{:S(2)}, u32[]{:S(2)}) async-start(bf16[4,64,1]{1,2,0:T(2,128)(2,1)} %all_to_all.12), calls=%async_computation.1 | async-start | bytes 4096 | tf_op jit(solution)/shard_map/all_to_all | solution.py:58
  71.0 404.4 %all-to-all-start = ((bf16[256,280,128]{2,1,0:T(8,128)(2,1)}), bf16[256,280,128]{2,1,0:T(8,128)(2,1)}, u32[]{:S(2)}, u32[]{:S(2)}) async-start(bf16[256,280,128]{2,1,0:T(8,128)(2,1)} %scatter_fusion), calls=%async_computation | async-start | bytes 36700160 | tf_op jit(solution)/shard_map/all_to_all | solution.py:57
  488.7 14.1 %collective-permute-start = (f32[280,512]{1,0:T(8,128)S(1)}, f32[280,512]{1,0:T(8,128)S(1)}, u32[]{:S(2)}, u32[]{:S(2)}) collective-permute-start(f32[280,512]{1,0:T(8,128)S(1)} %fusion.10), channel_id=1, source_target_pairs={{0,4},{4,0},{8,12},{12,8},{1,5},{5,1},{9,13},{13,9},{2,6},{6,2},{1... | collective-permute-start | bytes 1720328 | tf_op jit(solution)/shard_map/ppermute | solution.py:15
  502.8 26.4 %collective-permute-start.1 = (f32[280,512]{1,0:T(8,128)S(1)}, f32[280,512]{1,0:T(8,128)S(1)}, u32[]{:S(2)}, u32[]{:S(2)}) collective-permute-start(f32[280,512]{1,0:T(8,128)S(1)} %add.30), channel_id=1, source_target_pairs={{0,8},{4,12},{8,0},{12,4},{1,9},{5,13},{9,1},{13,5},{2,10},{6,14},... | collective-permute-start | bytes 1720328 | tf_op jit(solution)/shard_map/ppermute | solution.py:15
